TPU v7x, 32 devices: a whole 2x2x4 slice. The times are simulated.
32 devices in a mesh: groups: 2 (over y), seq: 16 (over z, x, core).
Axes of the slice: x: 2, y: 2, z: 4, core: 2. Of those that a mesh axis runs over, the one named last changes fastest.
Arguments:
- queries: bfloat16 [4096, 3072], P(('groups', 'seq')), parts along dimension 0, may hold values from -8 to 8
- keys: bfloat16 [4096, 3072], P(('groups', 'seq')), parts along dimension 0, may hold values from -6 to 6
- values: bfloat16 [4096, 3072], P(('groups', 'seq')), parts along dimension 0, may hold values from -6 to 6
- rand_blocks: int32 [32, 3], P('groups'), parts along dimension 0, may hold values from 0 to 15, as said below
- global_ids: int32 [4], P('groups'), parts along dimension 0, may hold values from 0 to 15, as said below
Outputs:
- attended: bfloat16 [4096, 3072], P(('groups', 'seq')), parts along dimension 0
There are 2 independent parts, one for each index of `groups`. A program takes and returns all parts, laid end to end along the dimension named above; each array names one. Nothing has to cross between parts.
Inputs may be any that keep to these rules, and one draw needn't show every extreme that they name: `rand_blocks`: row b names 3 different blocks, none of them b-1, b, b+1 or a global block. `global_ids`: 2 different blocks, one of which is the last block.
All inputs are finite; a program needn't handle non-finite values.
Results may differ from a plain program's by a relative error of at most 0.0049.
Values may be sent and summed in bfloat16 or wider, within the bound.
A program may use at most 128 MiB of HBM per device.

v0:
```python
from functools import reduce
import jax
import jax.numpy as jnp
from jax import lax
from jax.sharding import PartitionSpec as P

HEADS = 24
HEAD_DIM = 128
BLOCK = 128
GLOBALS = 2
RANDOMS = 3


def padded_2(cells, sides, width):
    for axis, dim in sides:
        count = lax.axis_size(axis)
        ends = count - 1
        head = lax.slice_in_dim(cells, 0, width, axis=dim)
        tail = lax.slice_in_dim(cells, cells.shape[dim] - width, cells.shape[dim], axis=dim)
        cells = jnp.concatenate(
            [
                lax.ppermute(tail, axis, [(i, (i + 1) % count) for i in range(ends)]),
                cells,
                lax.ppermute(head, axis, [((i + 1) % count, i) for i in range(ends)]),
            ],
            axis=dim,
        )
    return cells


def broadcast(array, axis, root):
    mine = lax.axis_index(axis) == root
    return lax.psum(jnp.where(mine, array, jnp.zeros_like(array)), axis)


def is_global(block_ids, global_ids):
    return jnp.any(block_ids[:, None] == global_ids[None, :], axis=1)


def local_scores(query_blocks, key_part, usable, scale):
    scores = (
        jnp.einsum("bqhd,bkhd->bhqk", query_blocks, key_part, preferred_element_type=jnp.float32)
        * scale
    )
    return jnp.where(usable[:, None, None, None], scores, -1e30)


def combine_parts(entries):
    maxima = [jnp.max(scores, axis=tuple(range(3, scores.ndim))) for scores, _, _ in entries]
    top = reduce(jnp.maximum, maxima)
    powers = [
        jnp.exp(scores - jnp.expand_dims(top, tuple(range(3, scores.ndim))))
        for scores, _, _ in entries
    ]
    total = reduce(jnp.add, [jnp.sum(power, axis=tuple(range(3, power.ndim))) for power in powers])
    pieces = []
    for power, entry in zip(powers, entries):
        probs = (power / jnp.expand_dims(total, tuple(range(3, power.ndim)))).astype(jnp.bfloat16)
        pieces.append(jnp.einsum(entry[2], probs, entry[1], preferred_element_type=jnp.float32))
    return reduce(jnp.add, pieces)


def local(queries, keys, values, rand_blocks, global_ids):
    length, width = queries.shape
    blocks_here = length // BLOCK
    block_count = rand_blocks.shape[0]
    scale = HEAD_DIM ** (-0.5)
    my_index = lax.axis_index("seq")
    block_ids = my_index * blocks_here + jnp.arange(blocks_here, dtype=jnp.int32)
    query_blocks = queries.reshape(blocks_here, BLOCK, HEADS, HEAD_DIM)
    near_keys = keys.reshape(blocks_here, BLOCK, HEADS, HEAD_DIM)
    near_values = values.reshape(blocks_here, BLOCK, HEADS, HEAD_DIM)
    stacked = jnp.stack([keys, values])
    key_slab, value_slab = (
        lax.all_to_all(keys.T, "seq", split_axis=0, concat_axis=1, tiled=True),
        lax.all_to_all(values.T, "seq", split_axis=0, concat_axis=1, tiled=True),
    )
    slab_width = key_slab.shape[0]
    key_slab = key_slab.reshape(slab_width, block_count, BLOCK)
    value_slab = value_slab.reshape(slab_width, block_count, BLOCK)
    prev_ok = (block_ids >= 1) & jnp.logical_not(is_global(block_ids - 1, global_ids))
    next_ok = (block_ids + 1 < block_count) & jnp.logical_not(is_global(block_ids + 1, global_ids))
    own_ok = jnp.logical_not(is_global(block_ids, global_ids))
    far_ok = jnp.ones((blocks_here, RANDOMS), dtype=bool)
    slots = rand_blocks.shape[1]
    picked_keys = jnp.take(key_slab, rand_blocks, axis=1)
    picked_values = jnp.take(value_slab, rand_blocks, axis=1)
    fetched_keys, fetched_values = (
        lax.all_to_all(picked_keys, "seq", split_axis=1, concat_axis=0, tiled=True),
        lax.all_to_all(picked_values, "seq", split_axis=1, concat_axis=0, tiled=True),
    )
    far_keys = fetched_keys.reshape(HEADS, HEAD_DIM, blocks_here, slots, BLOCK)
    far_values = fetched_values.reshape(HEADS, HEAD_DIM, blocks_here, slots, BLOCK)
    entries = [
        (local_scores(query_blocks, near_keys, own_ok, scale), near_values, "bhqk,bkhd->bqhd")
    ]
    far_scores = (
        jnp.einsum("bqhd,hdbsk->bhqsk", query_blocks, far_keys, preferred_element_type=jnp.float32)
        * scale
    )
    far_scores = jnp.where(far_ok[:, None, None, :, None], far_scores, -1e30)
    entries.append((far_scores, far_values, "bhqsk,hdbsk->bqhd"))
    padded = padded_2(stacked, (("seq", 1),), BLOCK)
    edge_blocks = padded.reshape(2, blocks_here + 2, BLOCK, HEADS, HEAD_DIM)
    entries.append(
        (
            local_scores(query_blocks, edge_blocks[0, :blocks_here], prev_ok, scale),
            edge_blocks[1, :blocks_here],
            "bhqk,bkhd->bqhd",
        )
    )
    entries.append(
        (
            local_scores(query_blocks, edge_blocks[0, 2:], next_ok, scale),
            edge_blocks[1, 2:],
            "bhqk,bkhd->bqhd",
        )
    )
    panels = []
    for slot_index in range(GLOBALS):
        chosen = global_ids[slot_index]
        panels.append(broadcast(stacked, "seq", chosen // blocks_here))
    panel = jnp.stack(panels)
    global_keys = panel[:, 0].reshape(GLOBALS, BLOCK, HEADS, HEAD_DIM)
    global_values = panel[:, 1].reshape(GLOBALS, BLOCK, HEADS, HEAD_DIM)
    global_scores = (
        jnp.einsum(
            "bqhd,gkhd->bhqgk", query_blocks, global_keys, preferred_element_type=jnp.float32
        )
        * scale
    )
    entries.append((global_scores, global_values, "bhqgk,gkhd->bqhd"))
    result = combine_parts(entries)
    return result.reshape(length, width).astype(jnp.bfloat16)


def solution(mesh):
    placed = (
        P(("groups", "seq"), None),
        P(("groups", "seq"), None),
        P(("groups", "seq"), None),
        P("groups", None),
        P("groups"),
    )
    return jax.shard_map(
        local, mesh=mesh, in_specs=placed, out_specs=P(("groups", "seq"), None), check_vma=False
    )
```

profile of v0, /device:TPU:10, one launch (start us, length us, event | category | flops | bytes accessed | tf_op | source)
XLA Modules:
  0.0 295.0 jit_solution(17898825059002964823)
XLA Ops:
  6.5 2.4 copy.38
  8.9 6.2 %all-to-all-start.2 = ((bf16[16,192,128]{2,1,0:T(8,128)(2,1)}), bf16[16,192,128]{2,1,0:T(8,128)(2,1)S(1)}, u32[]{:S(2)}, u32[]{:S(2)}) async-start(bf16[16,192,128]{2,1,0:T(8,128)(2,1)} %bitcast.29), calls=%async_computation.2 | async-start | bytes 1572864 | tf_op jit(solution)/shard_map/all_to_all | solution.py:76
  16.4 17.9 %all-to-all-done.2 = bf16[16,192,128]{2,1,0:T(8,128)(2,1)S(1)} async-done(((bf16[16,192,128]{2,1,0:T(8,128)(2,1)}), bf16[16,192,128]{2,1,0:T(8,128)(2,1)S(1)}, u32[]{:S(2)}, u32[]{:S(2)}) %all-to-all-start.2) | async-done | bytes 786464 | tf_op jit(solution)/shard_map/all_to_all | solution.py:76
  34.2 5.1 %all-to-all-start = ((bf16[16,192,128]{2,1,0:T(8,128)(2,1)}), bf16[16,192,128]{2,1,0:T(8,128)(2,1)S(1)}, u32[]{:S(2)}, u32[]{:S(2)}) async-start(bf16[16,192,128]{2,1,0:T(8,128)(2,1)} %bitcast.1), calls=%async_computation | async-start | bytes 1572864 | tf_op jit(solution)/shard_map/all_to_all | solution.py:75
  39.6 2.3 gather_fusion.1
  42.0 16.4 %all-to-all-done = bf16[16,192,128]{2,1,0:T(8,128)(2,1)S(1)} async-done(((bf16[16,192,128]{2,1,0:T(8,128)(2,1)}), bf16[16,192,128]{2,1,0:T(8,128)(2,1)S(1)}, u32[]{:S(2)}, u32[]{:S(2)}) %all-to-all-start) | async-done | bytes 786464 | tf_op jit(solution)/shard_map/all_to_all | solution.py:75
  58.4 2.3 gather_fusion
  60.7 5.1 %select_bitcast_fusion = (bf16[192,16,3,128]{3,0,2,1:T(8,128)(2,1)}, bf16[192,16,3,128]{3,0,2,1:T(8,128)(2,1)}) fusion(bf16[16,3,192,128]{3,2,1,0:T(8,128)(2,1)} %bitcast.170, pred[16,3]{1,0:T(8,128)(4,1)S(1)} %copy.31, bf16[16,3,192,128]{3,2,1,0:T(8,128)(2,1)} %bitcast.171), kind=kLoop, calls=%fused_computation.19 | loop fusion | flops 2359296 | bytes 9437232 | tf_op jit(solution)/shard_map/jit(_take)/select_n | solution.py:87
  65.8 5.2 %all-to-all-start.1 = ((bf16[192,16,3,128]{3,0,2,1:T(8,128)(2,1)}), bf16[192,16,3,128]{3,0,2,1:T(8,128)(2,1)S(1)}, u32[]{:S(2)}, u32[]{:S(2)}) async-start(bf16[192,16,3,128]{3,0,2,1:T(8,128)(2,1)} %get-tuple-element.24), calls=%async_computation.1 | async-start | bytes 4718592 | tf_op jit(solution)/shard_map/all_to_all | solution.py:89
  72.9 3.8 %pad_maximum_fusion.2 = (bf16[2,128,3072]{1,2,0:T(8,128)(2,1)}, bf16[1,2,128,3072]{2,3,0,1:T(8,128)(2,1)}, bf16[1,2,128,3072]{2,3,1,0:T(8,128)(2,1)}) fusion(bf16[1,128,3072]{1,2,0:T(8,128)(2,1)} %bitcast.11, bf16[1,128,3072]{1,2,0:T(8,128)(2,1)} %bitcast.10, pred[]{:T(512)S(6)} %eq.40, pred[]{:T(512)S(6)} %eq.39), kind=kLoop, calls=%fused_computation.23 | loop fusion | flops 2359296 | bytes 6291458 | tf_op jit(solution)/shard_map/stack | solution.py:73
  84.8 3.2 %fusion.43 = (f32[24,128]{1,0:T(8,128)S(1)}, f32[24,128,128]{1,2,0:T(8,128)}) fusion(pred[]{:T(512)S(6)} %not.12, bf16[128,3072]{1,0:T(8,128)(2,1)} %param.8, bf16[128,3072]{1,0:T(8,128)(2,1)} %param.7), kind=kOutput, calls=%fused_computation.81 | convolution fusion | flops 101839872 | bytes 3158017 | tf_op jit(solution)/shard_map/bqhd,bkhd->bhqk/dot_general | solution.py:42
  88.0 25.4 %collective-permute-done.1 = bf16[2,128,3072]{1,2,0:T(8,128)(2,1)} collective-permute-done((bf16[2,128,3072]{1,2,0:T(8,128)(2,1)}, bf16[2,128,3072]{1,2,0:T(8,128)(2,1)}, u32[]{:S(2)}, u32[]{:S(2)}) %collective-permute-start.1) | collective-permute-done | bytes 1572896 | tf_op jit(solution)/shard_map/ppermute | solution.py:24
  113.4 6.1 %collective-permute-done = bf16[2,128,3072]{1,2,0:T(8,128)(2,1)} collective-permute-done((bf16[2,128,3072]{1,2,0:T(8,128)(2,1)}, bf16[2,128,3072]{1,2,0:T(8,128)(2,1)}, u32[]{:S(2)}, u32[]{:S(2)}) %collective-permute-start) | collective-permute-done | bytes 1572896 | tf_op jit(solution)/shard_map/ppermute | solution.py:22
  119.5 4.1 %pad_maximum_fusion = bf16[2,384,3072]{1,2,0:T(8,128)(2,1)} fusion(bf16[2,128,3072]{1,2,0:T(8,128)(2,1)} %collective-permute-done.1, bf16[1,128,3072]{1,2,0:T(8,128)(2,1)} %bitcast.11, bf16[1,128,3072]{1,2,0:T(8,128)(2,1)} %bitcast.10, bf16[2,128,3072]{1,2,0:T(8,128)(2,1)} %collective-permute-done), kind=kLoop, calls=%fused_computation.2 | loop fusion | flops 18874368 | bytes 9437184 | tf_op jit(solution)/shard_map/concatenate | solution.py:20
  123.6 6.7 %copy.39 = bf16[2,384,3072]{2,1,0:T(8,128)(2,1)} copy(bf16[2,384,3072]{1,2,0:T(8,128)(2,1)} %pad_maximum_fusion) | data formatting | bytes 9437184 | tf_op jit(solution)/shard_map/concatenate | solution.py:20
  130.3 3.7 %copy.89 = bf16[96,8,24,128]{3,2,1,0:T(8,128)(2,1)S(1)} copy(bf16[96,8,24,128]{3,1,2,0:T(8,128)(2,1)} %bitcast.168) | data formatting | bytes 9437184
  136.0 2.5 copy.85
  138.5 2.4 copy.84
  140.9 3.2 %bitcast_reduce_fusion.2 = (f32[24,128]{1,0:T(8,128)S(1)}, f32[24,128,128]{2,1,0:T(8,128)}) fusion(bf16[1,1,128,24,128]{4,3,2,1,0:T(8,128)(2,1)} %get-tuple-element.15, pred[]{:T(512)S(6)} %and.19, bf16[128,3072]{1,0:T(8,128)(2,1)} %param.7), kind=kOutput, calls=%fused_computation.34 | convolution fusion | flops 101839872 | bytes 3158017 | tf_op jit(solution)/shard_map/bqhd,bkhd->bhqk/dot_general | solution.py:42
  144.1 48.8 %all-to-all-start.3 = ((bf16[192,16,3,128]{3,0,2,1:T(8,128)(2,1)}), bf16[192,16,3,128]{3,0,2,1:T(8,128)(2,1)}, u32[]{:S(2)}, u32[]{:S(2)}) async-start(bf16[192,16,3,128]{3,0,2,1:T(8,128)(2,1)} %get-tuple-element.23), calls=%async_computation.3 | async-start | bytes 4718592 | tf_op jit(solution)/shard_map/all_to_all | solution.py:90
  193.0 3.3 %bitcast_reduce_fusion.3 = (f32[24,128]{1,0:T(8,128)S(1)}, f32[24,128,128]{2,1,0:T(8,128)}) fusion(bf16[1,1,128,24,128]{4,3,2,1,0:T(8,128)(2,1)} %get-tuple-element.16, pred[]{:T(512)S(6)} %and.18, bf16[128,3072]{1,0:T(8,128)(2,1)} %param.7), kind=kOutput, calls=%fused_computation.37 | convolution fusion | flops 101839872 | bytes 3158017 | tf_op jit(solution)/shard_map/bqhd,bkhd->bhqk/dot_general | solution.py:42
  196.3 66.0 %all-reduce.3.cloned.1.call-done = (bf16[1,2,128,3072]{2,3,0,1:T(8,128)(2,1)}, bf16[1,2,128,3072]{2,3,1,0:T(8,128)(2,1)}) async-done(((bf16[1,2,128,3072]{2,3,0,1:T(8,128)(2,1)}, bf16[1,2,128,3072]{2,3,1,0:T(8,128)(2,1)}), (bf16[1,2,128,3072]{2,3,0,1:T(8,128)(2,1)}, bf16[1,2,128,3072]{2,3,1,0:T(8,128)(2,1)})) %all-reduce.3.cloned.1.call-update) | async-done | bytes 3145744 | tf_op jit(solution)/shard_map/psum | solution.py:33
  275.1 2.7 fusion.35
  283.0 3.9 %fusion.9 = bf16[1,128,24,128]{1,3,2,0:T(8,128)(2,1)S(1)} fusion(f32[24,128,128,1]{2,1,0,3:T(8,128)S(1)} %copy-done.11, f32[24,128,128]{2,1,0:T(8,128)S(1)} %fusion.29, f32[24,128,128]{2,1,0:T(8,128)S(1)} %copy-done.9, f32[24,128,128]{1,2,0:T(8,128)S(1)} %copy-done.10, bf16[24,128,3,128]{3,1,0,2:T(8,128)(2,1)S(1)} %bitcast.177, ...), kind=kOutput, calls=%fused_computation.25 | convolution fusion | flops 308674560 | bytes 14180352 | tf_op jit(solution)/shard_map/bhqsk,hdbsk->bqhd/dot_general | solution.py:59
  (55 shorter events, 29.4 us)
Async XLA Ops:
  6.5 8.6 %copy-start.4 = (bf16[128,3072]{1,0:T(8,128)(2,1)S(1)}, bf16[128,3072]{1,0:T(8,128)(2,1)}, u32[]{:S(2)}) copy-start(bf16[128,3072]{1,0:T(8,128)(2,1)} %param.8) | copy-start | bytes 2359300
  8.9 25.3 %all-to-all-start.2 = ((bf16[16,192,128]{2,1,0:T(8,128)(2,1)}), bf16[16,192,128]{2,1,0:T(8,128)(2,1)S(1)}, u32[]{:S(2)}, u32[]{:S(2)}) async-start(bf16[16,192,128]{2,1,0:T(8,128)(2,1)} %bitcast.29), calls=%async_computation.2 | async-start | bytes 1572864 | tf_op jit(solution)/shard_map/all_to_all | solution.py:76
  15.1 24.2 %copy-start.7 = (s32[16,3]{0,1:T(4,128)S(1)}, s32[16,3]{0,1:T(4,128)}, u32[]{:S(2)}) copy-start(s32[16,3]{0,1:T(4,128)} %param.10) | copy-start | bytes 580
  34.2 24.2 %all-to-all-start = ((bf16[16,192,128]{2,1,0:T(8,128)(2,1)}), bf16[16,192,128]{2,1,0:T(8,128)(2,1)S(1)}, u32[]{:S(2)}, u32[]{:S(2)}) async-start(bf16[16,192,128]{2,1,0:T(8,128)(2,1)} %bitcast.1), calls=%async_computation | async-start | bytes 1572864 | tf_op jit(solution)/shard_map/all_to_all | solution.py:75
  65.8 5.3 %copy-start.8 = (s32[2]{0:T(128)S(1)}, s32[2]{0:T(128)}, u32[]{:S(2)}) copy-start(s32[2]{0:T(128)} %param.11) | copy-start | bytes 28
  65.8 78.3 %all-to-all-start.1 = ((bf16[192,16,3,128]{3,0,2,1:T(8,128)(2,1)}), bf16[192,16,3,128]{3,0,2,1:T(8,128)(2,1)S(1)}, u32[]{:S(2)}, u32[]{:S(2)}) async-start(bf16[192,16,3,128]{3,0,2,1:T(8,128)(2,1)} %get-tuple-element.24), calls=%async_computation.1 | async-start | bytes 4718592 | tf_op jit(solution)/shard_map/all_to_all | solution.py:89
  71.1 191.2 %all-reduce.3.cloned.1.call-start = ((), (), s32[]{:S(2)}) async-start(), calls=%async_computation.4 | async-start | bytes 6291456 | tf_op jit(solution)/shard_map/psum | solution.py:33
  76.7 36.7 %collective-permute-start.1 = (bf16[2,128,3072]{1,2,0:T(8,128)(2,1)}, bf16[2,128,3072]{1,2,0:T(8,128)(2,1)}, u32[]{:S(2)}, u32[]{:S(2)}) collective-permute-start(bf16[2,128,3072]{1,2,0:T(8,128)(2,1)} %get-tuple-element.20), channel_id=1, source_target_pairs={{1,0},{2,1},{3,2},{4,3},{5,4},{6,5},{7,6},{8,7},{9,8},{10,9},{11,1... | collective-permute-start | bytes 4718600 | tf_op jit(solution)/shard_map/ppermute | solution.py:24
  78.9 40.6 %collective-permute-start = (bf16[2,128,3072]{1,2,0:T(8,128)(2,1)}, bf16[2,128,3072]{1,2,0:T(8,128)(2,1)}, u32[]{:S(2)}, u32[]{:S(2)}) collective-permute-start(bf16[2,128,3072]{1,2,0:T(8,128)(2,1)} %get-tuple-element.20), channel_id=1, source_target_pairs={{0,1},{1,2},{2,3},{3,4},{4,5},{5,6},{6,7},{7,8},{8,9},{9,10},{10,1... | collective-permute-start | bytes 4718600 | tf_op jit(solution)/shard_map/ppermute | solution.py:22
  144.1 135.8 %all-to-all-start.3 = ((bf16[192,16,3,128]{3,0,2,1:T(8,128)(2,1)}), bf16[192,16,3,128]{3,0,2,1:T(8,128)(2,1)}, u32[]{:S(2)}, u32[]{:S(2)}) async-start(bf16[192,16,3,128]{3,0,2,1:T(8,128)(2,1)} %get-tuple-element.23), calls=%async_computation.3 | async-start | bytes 4718592 | tf_op jit(solution)/shard_map/all_to_all | solution.py:90
  265.3 1.6 copy-start.3
  266.3 4.9 %copy-start = (f32[24,3,128,128]{3,2,1,0:T(8,128)}, f32[24,3,128,128]{3,2,1,0:T(8,128)S(1)}, u32[]{:S(2)}) copy-start(f32[24,3,128,128]{3,2,1,0:T(8,128)S(1)} %get-tuple-element.36) | copy-start | bytes 14155780
  266.4 2.7 copy-start.1
  266.4 3.7 %copy-start.2 = (f32[24,128,128]{2,1,0:T(8,128)S(1)}, f32[24,128,128]{2,1,0:T(8,128)}, u32[]{:S(2)}) copy-start(f32[24,128,128]{2,1,0:T(8,128)} %get-tuple-element.30) | copy-start | bytes 4718596
  271.2 1.1 copy-start.6
  272.3 1.1 copy-start.5
  280.0 2.1 copy-start.9
  280.0 2.6 copy-start.10
  280.0 3.1 %copy-start.11 = (f32[24,128,128,1]{2,1,0,3:T(8,128)S(1)}, f32[24,128,128,1]{2,1,0,3:T(8,128)}, u32[]{:S(2)}) copy-start(f32[24,128,128,1]{2,1,0,3:T(8,128)} %fusion.10) | copy-start | bytes 4718596
Sparse Core Ops, SparseCore 0:
  81.1 181.0 all-reduce.2
where the time goes:
time: 296 us; the launch traced here: 295 us
  waiting for transfers between devices  132 us (45%)
  starting transfers between devices  69.8 us (24%)
  local copies, waits for them, and re-layouts  36.2 us (12%)
  matrix products  22.4 us (8%)
  other arithmetic  18.3 us (6%)
  between operations  16.6 us (6%)
    psum x1, waiting for transfers between devices, broadcast(): return lax.psum(jnp.where(mine, array, jnp.zeros_like(array)), axis)  66 us
    all_to_all x1, starting transfers between devices, local(): lax.all_to_all(picked_values, 'seq', split_axis=1, concat_axis=0, tiled=T...  48.8 us
    ppermute x1, waiting for transfers between devices, padded_2(): lax.ppermute(head, axis, [((i + 1) % count, i) for i in range(ends)])  25.4 us
    unnamed x30, local copies, waits for them, and re-layouts  18.7 us
    all_to_all x1, waiting for transfers between devices, local(): lax.all_to_all(values.T, 'seq', split_axis=0, concat_axis=1, tiled=True)  17.9 us
    all_to_all x1, waiting for transfers between devices, local(): lax.all_to_all(keys.T, 'seq', split_axis=0, concat_axis=1, tiled=True)  16.4 us
    dot_general x5, matrix products, combine_parts(): jnp.einsum(entry[2], probs, entry[1], preferred_element_type=jnp.float32)  10.8 us
    dot_general x3, matrix products, local_scores(): jnp.einsum('bqhd,bkhd->bhqk', query_blocks, key_part, preferred_element_t...  9.77 us
  transfers between devices with their start and end apart: 7, of which 5 were waited for; matrix products, arithmetic and copies ran while one was open for 19% of the time, Pallas kernels for 0%

commit v1 on v0

--- a/solution.py
+++ b/solution.py
@@ -30,7 +30,7 @@
 
 def broadcast(array, axis, root):
     mine = lax.axis_index(axis) == root
-    return lax.psum(jnp.where(mine, array, jnp.zeros_like(array)), axis)
+    return jnp.sum(lax.all_gather(jnp.where(mine, array, jnp.zeros_like(array)), axis), axis=0)
 
 
 def is_global(block_ids, global_ids):

time: 296 us -> 459 us (1.55)
  waiting for transfers between devices: 132 us -> 236 us
  blocking collectives: 0 us -> 85.2 us
  starting transfers between devices: 69.8 us -> 26.4 us
  other arithmetic: 18.3 us -> 46.8 us
  local copies, waits for them, and re-layouts: 36.2 us -> 27.6 us
  matrix products: 22.4 us -> 17.2 us
    all_gather x0 -> x2, waiting for transfers between devices: none -> 130 us  [broadcast(): lax.all_gather(jnp.where(mine, array, jnp.zeros_like(array)), axis)]
    all_to_all x0 -> x1, blocking collectives: none -> 85.2 us  [local(): lax.all_to_all(picked_keys, 'seq', split_axis=1, concat_axis=0, tiled=True)]
    psum x1 -> x0, waiting for transfers between devices: 66 us -> none  [broadcast(): return lax.psum(jnp.where(mine, array, jnp.zeros_like(array)), axis)]
    all_to_all x1, starting transfers between devices: 48.8 us -> 8.14 us  [local(): lax.all_to_all(picked_values, 'seq', split_axis=1, concat_axis=0, tiled=T...]
    all_to_all x1, waiting for transfers between devices: 0.01 us -> 36.8 us  [local(): lax.all_to_all(picked_values, 'seq', split_axis=1, concat_axis=0, tiled=T...]
    reduce_sum x0 -> x2, other arithmetic: none -> 29.5 us  [broadcast(): jnp.sum(lax.all_gather(jnp.where(mine, array, jnp.zeros_like(array)), axi...]
    ppermute x1, waiting for transfers between devices: 25.4 us -> 16.7 us  [padded_2(): lax.ppermute(head, axis, [((i + 1) % count, i) for i in range(ends)])]
    all_to_all x1, waiting for transfers between devices: 16.4 us -> 25 us  [local(): lax.all_to_all(keys.T, 'seq', split_axis=0, concat_axis=1, tiled=True)]
  transfers between devices with their start and end apart: 7 -> 7, of which waited for: 5 -> 7; matrix products, arithmetic and copies ran while one was open for 19% -> 11% of each run, Pallas kernels for 0% -> 0%
where the time goes in v1:
time: 459 us; the launch traced here: 456 us
  waiting for transfers between devices  236 us (51%)
  blocking collectives  85.2 us (19%)
  other arithmetic  46.8 us (10%)
  local copies, waits for them, and re-layouts  27.6 us (6%)
  starting transfers between devices  26.4 us (6%)
  matrix products  17.2 us (4%)
  between operations  16.6 us (4%)
    all_gather x2, waiting for transfers between devices, broadcast(): lax.all_gather(jnp.where(mine, array, jnp.zeros_like(array)), axis)  130 us
    all_to_all x1, blocking collectives, local(): lax.all_to_all(picked_keys, 'seq', split_axis=1, concat_axis=0, tiled=True)  85.2 us
    all_to_all x1, waiting for transfers between devices, local(): lax.all_to_all(picked_values, 'seq', split_axis=1, concat_axis=0, tiled=T...  36.8 us
    reduce_sum x2, other arithmetic, broadcast(): jnp.sum(lax.all_gather(jnp.where(mine, array, jnp.zeros_like(array)), axi...  29.5 us
    all_to_all x1, waiting for transfers between devices, local(): lax.all_to_all(values.T, 'seq', split_axis=0, concat_axis=1, tiled=True)  26.3 us
    all_to_all x1, waiting for transfers between devices, local(): lax.all_to_all(keys.T, 'seq', split_axis=0, concat_axis=1, tiled=True)  25 us
    ppermute x1, waiting for transfers between devices, padded_2(): lax.ppermute(head, axis, [((i + 1) % count, i) for i in range(ends)])  16.7 us
    unnamed x39, local copies, waits for them, and re-layouts  10.6 us
  transfers between devices with their start and end apart: 7, of which 7 were waited for; matrix products, arithmetic and copies ran while one was open for 11% of the time, Pallas kernels for 0%

profile of v1, /device:TPU:10, one launch (start us, length us, event | category | flops | bytes accessed | tf_op | source)
XLA Modules:
  0.0 456.2 jit_solution(16893273621224134790)
XLA Ops:
  9.1 3.3 broadcast_select_fusion.1
  14.7 6.2 %all-to-all-start.2 = ((bf16[16,192,128]{2,1,0:T(8,128)(2,1)}), bf16[16,192,128]{2,1,0:T(8,128)(2,1)S(1)}, u32[]{:S(2)}, u32[]{:S(2)}) async-start(bf16[16,192,128]{2,1,0:T(8,128)(2,1)} %bitcast.30), calls=%async_computation.2 | async-start | bytes 1572864 | tf_op jit(solution)/shard_map/all_to_all | solution.py:76
  22.1 26.3 %all-to-all-done.2 = bf16[16,192,128]{2,1,0:T(8,128)(2,1)S(1)} async-done(((bf16[16,192,128]{2,1,0:T(8,128)(2,1)}), bf16[16,192,128]{2,1,0:T(8,128)(2,1)S(1)}, u32[]{:S(2)}, u32[]{:S(2)}) %all-to-all-start.2) | async-done | bytes 786464 | tf_op jit(solution)/shard_map/all_to_all | solution.py:76
  48.4 7.4 %all-to-all-start = ((bf16[16,192,128]{2,1,0:T(8,128)(2,1)}), bf16[16,192,128]{2,1,0:T(8,128)(2,1)S(1)}, u32[]{:S(2)}, u32[]{:S(2)}) async-start(bf16[16,192,128]{2,1,0:T(8,128)(2,1)} %bitcast.186), calls=%async_computation | async-start | bytes 1572864 | tf_op jit(solution)/shard_map/all_to_all | solution.py:75
  56.1 2.4 gather_fusion.1
  58.5 25.0 %all-to-all-done = bf16[16,192,128]{2,1,0:T(8,128)(2,1)S(1)} async-done(((bf16[16,192,128]{2,1,0:T(8,128)(2,1)}), bf16[16,192,128]{2,1,0:T(8,128)(2,1)S(1)}, u32[]{:S(2)}, u32[]{:S(2)}) %all-to-all-start) | async-done | bytes 786464 | tf_op jit(solution)/shard_map/all_to_all | solution.py:75
  83.5 2.3 gather_fusion
  85.9 4.5 select_bitcast_fusion
  90.3 85.2 %all_to_all.62 = bf16[192,16,3,128]{3,0,2,1:T(8,128)(2,1)} all-to-all(bf16[192,16,3,128]{3,0,2,1:T(8,128)(2,1)S(1)} %get-tuple-element.21), channel_id=1, replica_groups=mesh['groups'=2,'seq'=16] {'seq'}, dimensions={1} | all-to-all | bytes 4718592 | tf_op jit(solution)/shard_map/all_to_all | solution.py:89
  175.5 8.1 %all-to-all-start.3 = ((bf16[192,16,3,128]{3,0,2,1:T(8,128)(2,1)}), bf16[192,16,3,128]{3,0,2,1:T(8,128)(2,1)}, u32[]{:S(2)}, u32[]{:S(2)}) async-start(bf16[192,16,3,128]{3,0,2,1:T(8,128)(2,1)} %get-tuple-element.20), calls=%async_computation.3 | async-start | bytes 4718592 | tf_op jit(solution)/shard_map/all_to_all | solution.py:90
  184.9 2.3 collective-permute-start.1
  187.3 2.3 collective-permute-start
  194.2 2.9 fusion.43
  197.2 16.7 %collective-permute-done.1 = bf16[2,128,3072]{2,1,0:T(8,128)(2,1)S(1)} collective-permute-done((bf16[2,128,3072]{2,1,0:T(8,128)(2,1)}, bf16[2,128,3072]{2,1,0:T(8,128)(2,1)S(1)}, u32[]{:S(2)}, u32[]{:S(2)}) %collective-permute-start.1) | collective-permute-done | bytes 1572896 | tf_op jit(solution)/shard_map/ppermute | solution.py:24
  225.2 36.8 %all-to-all-done.3 = bf16[192,16,3,128]{3,0,2,1:T(8,128)(2,1)} async-done(((bf16[192,16,3,128]{3,0,2,1:T(8,128)(2,1)}), bf16[192,16,3,128]{3,0,2,1:T(8,128)(2,1)}, u32[]{:S(2)}, u32[]{:S(2)}) %all-to-all-start.3) | async-done | bytes 2359328 | tf_op jit(solution)/shard_map/all_to_all | solution.py:90
  262.1 3.3 copy.80
  265.4 3.2 bitcast_reduce_fusion
  268.6 11.1 %all-gather.3.cloned.1.call-done = bf16[16,2,128,3072]{3,2,1,0:T(8,128)(2,1)} async-done(((bf16[1,2,128,3072]{3,2,1,0:T(8,128)(2,1)}), bf16[16,2,128,3072]{3,2,1,0:T(8,128)(2,1)}) %all-gather.3.cloned.1.call-update) | async-done | bytes 25165840 | tf_op jit(solution)/shard_map/all_gather | solution.py:33
  279.7 14.4 %reduce_sum.69 = bf16[2,128,3072]{2,1,0:T(8,128)(2,1)S(1)} reduce(bf16[16,2,128,3072]{3,2,1,0:T(8,128)(2,1)} %all-gather.3.cloned.1.call-done, bf16[]{:T(256)} %constant.57.clone.1), dimensions={0}, to_apply=%region_7.9 | reduce | flops 11796480 | bytes 26738690 | tf_op jit(solution)/shard_map/reduce_sum | solution.py:33
  294.2 118.4 %all-gather.5.cloned.1.call-done = bf16[16,2,128,3072]{3,2,1,0:T(8,128)(2,1)} async-done(((bf16[1,2,128,3072]{3,2,1,0:T(8,128)(2,1)}), bf16[16,2,128,3072]{3,2,1,0:T(8,128)(2,1)}) %all-gather.5.cloned.1.call-update) | async-done | bytes 25165840 | tf_op jit(solution)/shard_map/all_gather | solution.py:33
  412.6 15.1 %reduce_sum.70 = bf16[2,128,3072]{2,1,0:T(8,128)(2,1)} reduce(bf16[16,2,128,3072]{3,2,1,0:T(8,128)(2,1)} %all-gather.5.cloned.1.call-done, bf16[]{:T(256)} %constant.57.clone.1), dimensions={0}, to_apply=%region_8.10 | reduce | flops 11796480 | bytes 26738690 | tf_op jit(solution)/shard_map/reduce_sum | solution.py:33
  427.7 3.3 fusion.8
  431.0 2.7 copy.86
  435.3 2.3 bitcast_reduce_fusion.1
  (72 shorter events, 33.8 us)
Async XLA Ops:
  6.5 273.2 %all-gather.3.cloned.1.call-start = ((), (), s32[]{:S(2)}) async-start(), calls=%async_computation.4 | async-start | bytes 26738688 | tf_op jit(solution)/shard_map/all_gather | solution.py:33
  12.3 1.1 copy-start
  12.4 400.2 %all-gather.5.cloned.1.call-start = ((), (), s32[]{:S(2)}) async-start(), calls=%async_computation.5 | async-start | bytes 26738688 | tf_op jit(solution)/shard_map/all_gather | solution.py:33
  13.5 7.4 %copy-start.1 = (bf16[128,3072]{1,0:T(8,128)(2,1)S(1)}, bf16[128,3072]{1,0:T(8,128)(2,1)}, u32[]{:S(2)}) copy-start(bf16[128,3072]{1,0:T(8,128)(2,1)} %param.8) | copy-start | bytes 2359300
  14.7 33.7 %all-to-all-start.2 = ((bf16[16,192,128]{2,1,0:T(8,128)(2,1)}), bf16[16,192,128]{2,1,0:T(8,128)(2,1)S(1)}, u32[]{:S(2)}, u32[]{:S(2)}) async-start(bf16[16,192,128]{2,1,0:T(8,128)(2,1)} %bitcast.30), calls=%async_computation.2 | async-start | bytes 1572864 | tf_op jit(solution)/shard_map/all_to_all | solution.py:76
  20.9 34.9 %copy-start.13 = (s32[16,3]{0,1:T(4,128)S(1)}, s32[16,3]{0,1:T(4,128)}, u32[]{:S(2)}) copy-start(s32[16,3]{0,1:T(4,128)} %param.10) | copy-start | bytes 580
  48.4 35.1 %all-to-all-start = ((bf16[16,192,128]{2,1,0:T(8,128)(2,1)}), bf16[16,192,128]{2,1,0:T(8,128)(2,1)S(1)}, u32[]{:S(2)}, u32[]{:S(2)}) async-start(bf16[16,192,128]{2,1,0:T(8,128)(2,1)} %bitcast.186), calls=%async_computation | async-start | bytes 1572864 | tf_op jit(solution)/shard_map/all_to_all | solution.py:75
  175.5 86.6 %all-to-all-start.3 = ((bf16[192,16,3,128]{3,0,2,1:T(8,128)(2,1)}), bf16[192,16,3,128]{3,0,2,1:T(8,128)(2,1)}, u32[]{:S(2)}, u32[]{:S(2)}) async-start(bf16[192,16,3,128]{3,0,2,1:T(8,128)(2,1)} %get-tuple-element.20), calls=%async_computation.3 | async-start | bytes 4718592 | tf_op jit(solution)/shard_map/all_to_all | solution.py:90
  184.9 6.8 %copy-start.14 = (s32[2]{0:T(128)S(1)}, s32[2]{0:T(128)}, u32[]{:S(2)}) copy-start(s32[2]{0:T(128)} %param.11) | copy-start | bytes 28
  184.9 28.9 %collective-permute-start.1 = (bf16[2,128,3072]{2,1,0:T(8,128)(2,1)}, bf16[2,128,3072]{2,1,0:T(8,128)(2,1)S(1)}, u32[]{:S(2)}, u32[]{:S(2)}) collective-permute-start(bf16[2,128,3072]{2,1,0:T(8,128)(2,1)} %pad_maximum_fusion.2), channel_id=1, source_target_pairs={{1,0},{2,1},{3,2},{4,3},{5,4},{6,5},{7,6},{8,7},{9,8},{10,9},{11,1... | collective-permute-start | bytes 4718600 | tf_op jit(solution)/shard_map/ppermute | solution.py:24
  187.3 27.7 %collective-permute-start = (bf16[2,128,3072]{2,1,0:T(8,128)(2,1)}, bf16[2,128,3072]{2,1,0:T(8,128)(2,1)}, u32[]{:S(2)}, u32[]{:S(2)}) collective-permute-start(bf16[2,128,3072]{2,1,0:T(8,128)(2,1)} %pad_maximum_fusion.2), channel_id=1, source_target_pairs={{0,1},{1,2},{2,3},{3,4},{4,5},{5,6},{6,7},{7,8},{8,9},{9,10},{10,1... | collective-permute-start | bytes 4718600 | tf_op jit(solution)/shard_map/ppermute | solution.py:22
  220.0 1.4 copy-start.10
  223.2 1.9 copy-start.2
  262.1 3.3 copy-start.3
  431.0 2.7 copy-start.4
  433.7 4.5 slice-start
  435.3 2.9 slice-start.1
  438.2 1.4 copy-start.7
  438.3 1.9 copy-start.8
  438.3 2.3 copy-start.9
  440.6 1.4 copy-start.6
  442.0 1.1 copy-start.12
  443.1 1.1 copy-start.11
  444.7 1.9 copy-start.5
Sparse Core Ops, SparseCore 0:
  12.5 267.2 all-gather.2
  281.3 131.1 all-gather.4
